TPU v7x, 32 devices: a whole 2x2x4 slice. The times are simulated.
32 devices in a mesh: dp: 8 (over y, x, core), tensor: 4 (over z).
Axes of the slice: x: 2, y: 2, z: 4, core: 2. Of those that a mesh axis runs over, the one named last changes fastest.
Arguments:
- hidden_in: bfloat16 [16384, 768], P('dp'), may hold values from -6 to 6
- query_weight: bfloat16 [768, 768], P(None, 'tensor'), may hold values from -0.21875 to 0.21875
- query_bias: bfloat16 [768], P('tensor'), may hold values from -3 to 3
- key_weight: bfloat16 [768, 768], P(None, 'tensor'), may hold values from -0.21875 to 0.21875
- value_weight: bfloat16 [768, 768], P(None, 'tensor'), may hold values from -0.21875 to 0.21875
- value_bias: bfloat16 [768], P('tensor'), may hold values from -3 to 3
- output_weight: bfloat16 [768, 768], P('tensor'), may hold values from -2.5 to 2.5
- output_bias: bfloat16 [768], replicated, may hold values from -3 to 3
- attn_gain: bfloat16 [768], replicated, may hold values from 0.25 to 1.75
- attn_shift: bfloat16 [768], replicated, may hold values from -3 to 3
- up_weight: bfloat16 [768, 3072], P(None, 'tensor'), may hold values from -0.21875 to 0.21875
- up_bias: bfloat16 [3072], P('tensor'), may hold values from -3 to 3
- down_weight: bfloat16 [3072, 768], P('tensor'), may hold values from -0.109375 to 0.109375
- down_bias: bfloat16 [768], replicated, may hold values from -3 to 3
- ffn_gain: bfloat16 [768], replicated, may hold values from 0.25 to 1.75
- ffn_shift: bfloat16 [768], replicated, may hold values from -3 to 3
- cotangent: bfloat16 [16384, 768], P('dp'), may hold values from -6 to 6
Outputs:
- layer_out: bfloat16 [16384, 768], P('dp')
- input_grad: bfloat16 [16384, 768], P('dp')
- query_weight_grad: float32 [768, 768], P(None, 'tensor')
- query_bias_grad: float32 [768], P('tensor')
- key_weight_grad: float32 [768, 768], P(None, 'tensor')
- value_weight_grad: float32 [768, 768], P(None, 'tensor')
- value_bias_grad: float32 [768], P('tensor')
- output_weight_grad: float32 [768, 768], P('tensor')
- output_bias_grad: float32 [768], replicated
- attn_gain_grad: float32 [768], replicated
- attn_shift_grad: float32 [768], replicated
- up_weight_grad: float32 [768, 3072], P(None, 'tensor')
- up_bias_grad: float32 [3072], P('tensor')
- down_weight_grad: float32 [3072, 768], P('tensor')
- down_bias_grad: float32 [768], replicated
- ffn_gain_grad: float32 [768], replicated
- ffn_shift_grad: float32 [768], replicated
All inputs are finite; a program needn't handle non-finite values.
Results may differ from a plain program's by a relative error of at most 0.023.
Values may be sent and summed in bfloat16 or wider, within the bound.
No kernel may reach another device: no remote copies, remote signals or barrier semaphores. Data moves between devices by JAX's collectives and lax.ppermute only.
A program may use at most 192 MiB of HBM per device.

v0:
```python
import jax
import jax.numpy as jnp
from jax import lax
from jax.sharding import PartitionSpec as P

LEN = 512
HDIM = 64


epsilon = 1e-12
root_half = 0.7071067811865476
density_norm = 0.3989422804014327


def norm_parts(values):
    center = values - jnp.mean(values, axis=-1, keepdims=True)
    inverse = lax.rsqrt(jnp.mean(center * center, axis=-1, keepdims=True) + epsilon)
    return (center * inverse, inverse[:, 0])


def norm_back(grad_out, normal, inverse, norm_gain):
    scaled = grad_out * norm_gain.astype(jnp.float32)
    first_mean = jnp.mean(scaled, axis=-1, keepdims=True)
    cross_mean = jnp.mean(scaled * normal, axis=-1, keepdims=True)
    return inverse[:, None] * (scaled - first_mean - normal * cross_mean)


def column_product(left, right):
    return lax.dot_general(
        left, right, (((0,), (0,)), ((), ())), preferred_element_type=jnp.float32
    )


def back_product(left, right):
    return lax.dot_general(
        left, right, (((1,), (1,)), ((), ())), preferred_element_type=jnp.float32
    )


def gelu_slope(values):
    return (
        0.5 * (1.0 + lax.erf(values * root_half))
        + values * jnp.exp(-0.5 * values * values) * density_norm
    )


def column_total(values):
    return jnp.sum(values, axis=0, dtype=jnp.float32)


def shards(
    hidden_in,
    query_weight,
    query_bias,
    key_weight,
    value_weight,
    value_bias,
    output_weight,
    output_bias,
    attn_gain,
    attn_shift,
    up_weight,
    up_bias,
    down_weight,
    down_bias,
    ffn_gain,
    ffn_shift,
    cotangent,
):
    row_count = hidden_in.shape[0]
    seq_count = row_count // LEN
    group_width = query_weight.shape[1]
    group_heads = group_width // HDIM
    score_scale = HDIM ** (-0.5)
    head_shape = (seq_count, LEN, group_heads, HDIM)
    inputs = hidden_in.astype(jnp.float32)
    queries = (
        jnp.dot(hidden_in, query_weight, preferred_element_type=jnp.float32)
        + query_bias.astype(jnp.float32)
    ).astype(jnp.bfloat16)
    key_rows = jnp.dot(hidden_in, key_weight, preferred_element_type=jnp.float32).astype(
        jnp.bfloat16
    )
    value_rows = (
        jnp.dot(hidden_in, value_weight, preferred_element_type=jnp.float32)
        + value_bias.astype(jnp.float32)
    ).astype(jnp.bfloat16)
    query_heads = queries.reshape(head_shape)
    key_heads = key_rows.reshape(head_shape)
    value_heads = value_rows.reshape(head_shape)
    scores = (
        jnp.einsum("bqhd,bkhd->bhqk", query_heads, key_heads, preferred_element_type=jnp.float32)
        * score_scale
    )
    row_peak = jnp.max(scores, axis=-1, keepdims=True)
    exp_scores = jnp.exp(scores - row_peak)
    exp_total = jnp.sum(exp_scores, axis=-1, keepdims=True)
    attn_probs = (exp_scores / exp_total).astype(jnp.bfloat16)
    log_total = row_peak + jnp.log(exp_total)
    mixed_rows = jnp.einsum(
        "bhqk,bkhd->bqhd", attn_probs, value_heads, preferred_element_type=jnp.float32
    )
    mixed_rows = mixed_rows.reshape(row_count, group_width).astype(jnp.bfloat16)
    attn_part = jnp.dot(mixed_rows, output_weight, preferred_element_type=jnp.float32)
    attn_total = lax.psum(attn_part.astype(jnp.bfloat16), "tensor").astype(jnp.float32)
    normal_attn, inverse_attn = norm_parts(inputs + attn_total + output_bias.astype(jnp.float32))
    normed = normal_attn * attn_gain.astype(jnp.float32) + attn_shift.astype(jnp.float32)
    ffn_source = normed.astype(jnp.bfloat16)
    pre_act = jnp.dot(ffn_source, up_weight, preferred_element_type=jnp.float32) + up_bias.astype(
        jnp.float32
    )
    active = jax.nn.gelu(pre_act, approximate=False).astype(jnp.bfloat16)
    ffn_part = jnp.dot(active, down_weight, preferred_element_type=jnp.float32)
    ffn_total = lax.psum(ffn_part.astype(jnp.bfloat16), "tensor").astype(jnp.float32)
    normal_ffn, inverse_ffn = norm_parts(normed + ffn_total + down_bias.astype(jnp.float32))
    layer_out = (normal_ffn * ffn_gain.astype(jnp.float32) + ffn_shift.astype(jnp.float32)).astype(
        jnp.bfloat16
    )
    grad_out = cotangent.astype(jnp.float32)
    ffn_gain_grad = column_total(grad_out * normal_ffn)
    ffn_shift_grad = column_total(grad_out)
    grad_second = norm_back(grad_out, normal_ffn, inverse_ffn, ffn_gain)
    down_bias_grad = column_total(grad_second)
    second_low = grad_second.astype(jnp.bfloat16)
    down_weight_grad = column_product(active, second_low)
    grad_active = back_product(second_low, down_weight)
    grad_pre = (grad_active * gelu_slope(pre_act)).astype(jnp.bfloat16)
    up_bias_grad = column_total(grad_pre)
    up_weight_grad = column_product(ffn_source, grad_pre)
    normed_part = back_product(grad_pre, up_weight)
    normed_total = lax.psum(normed_part.astype(jnp.bfloat16), "tensor").astype(jnp.float32)
    grad_first = grad_second + normed_total
    attn_gain_grad = column_total(grad_first * normal_attn)
    attn_shift_grad = column_total(grad_first)
    grad_resid = norm_back(grad_first, normal_attn, inverse_attn, attn_gain)
    output_bias_grad = column_total(grad_resid)
    resid_low = grad_resid.astype(jnp.bfloat16)
    output_weight_grad = column_product(mixed_rows, resid_low)
    grad_context = back_product(resid_low, output_weight).astype(jnp.bfloat16).reshape(head_shape)
    scores_again = (
        jnp.einsum("bqhd,bkhd->bhqk", query_heads, key_heads, preferred_element_type=jnp.float32)
        * score_scale
    )
    probs_full = jnp.exp(scores_again - log_total)
    probs_low = probs_full.astype(jnp.bfloat16)
    value_grad_rows = jnp.einsum(
        "bhqk,bqhd->bkhd", probs_low, grad_context, preferred_element_type=jnp.float32
    )
    value_grad_rows = value_grad_rows.reshape(row_count, group_width).astype(jnp.bfloat16)
    grad_probs = jnp.einsum(
        "bqhd,bkhd->bhqk", grad_context, value_heads, preferred_element_type=jnp.float32
    )
    inner_sum = jnp.sum(probs_full * grad_probs, axis=-1, keepdims=True)
    grad_scores = (probs_full * (grad_probs - inner_sum)).astype(jnp.bfloat16)
    query_grad_rows = jnp.einsum(
        "bhqk,bkhd->bqhd", grad_scores, key_heads, preferred_element_type=jnp.float32
    )
    query_grad_rows = (
        (query_grad_rows * score_scale).reshape(row_count, group_width).astype(jnp.bfloat16)
    )
    key_grad_rows = jnp.einsum(
        "bhqk,bqhd->bkhd", grad_scores, query_heads, preferred_element_type=jnp.float32
    )
    key_grad_rows = (
        (key_grad_rows * score_scale).reshape(row_count, group_width).astype(jnp.bfloat16)
    )
    query_bias_grad = column_total(query_grad_rows)
    value_bias_grad = column_total(value_grad_rows)
    query_weight_grad = column_product(hidden_in, query_grad_rows)
    key_weight_grad = column_product(hidden_in, key_grad_rows)
    value_weight_grad = column_product(hidden_in, value_grad_rows)
    input_part = (
        back_product(query_grad_rows, query_weight)
        + back_product(key_grad_rows, key_weight)
        + back_product(value_grad_rows, value_weight)
    )
    input_total = lax.psum(input_part.astype(jnp.bfloat16), "tensor").astype(jnp.float32)
    input_grad = (grad_resid + input_total).astype(jnp.bfloat16)
    (
        query_weight_grad,
        query_bias_grad,
        key_weight_grad,
        value_weight_grad,
        value_bias_grad,
        output_weight_grad,
        output_bias_grad,
        attn_gain_grad,
        attn_shift_grad,
        up_weight_grad,
        up_bias_grad,
        down_weight_grad,
        down_bias_grad,
        ffn_gain_grad,
        ffn_shift_grad,
    ) = lax.psum(
        (
            query_weight_grad,
            query_bias_grad,
            key_weight_grad,
            value_weight_grad,
            value_bias_grad,
            output_weight_grad,
            output_bias_grad,
            attn_gain_grad,
            attn_shift_grad,
            up_weight_grad,
            up_bias_grad,
            down_weight_grad,
            down_bias_grad,
            ffn_gain_grad,
            ffn_shift_grad,
        ),
        "dp",
    )
    return (
        layer_out,
        input_grad,
        query_weight_grad,
        query_bias_grad,
        key_weight_grad,
        value_weight_grad,
        value_bias_grad,
        output_weight_grad,
        output_bias_grad,
        attn_gain_grad,
        attn_shift_grad,
        up_weight_grad,
        up_bias_grad,
        down_weight_grad,
        down_bias_grad,
        ffn_gain_grad,
        ffn_shift_grad,
    )


def solution(mesh):
    in_specs = (
        P("dp", None),
        P(None, "tensor"),
        P("tensor"),
        P(None, "tensor"),
        P(None, "tensor"),
        P("tensor"),
        P("tensor", None),
        P(),
        P(),
        P(),
        P(None, "tensor"),
        P("tensor"),
        P("tensor", None),
        P(),
        P(),
        P(),
        P("dp", None),
    )
    out_specs = (
        P("dp", None),
        P("dp", None),
        P(None, "tensor"),
        P("tensor"),
        P(None, "tensor"),
        P(None, "tensor"),
        P("tensor"),
        P("tensor", None),
        P(),
        P(),
        P(),
        P(None, "tensor"),
        P("tensor"),
        P("tensor", None),
        P(),
        P(),
        P(),
    )
    return jax.shard_map(shards, mesh=mesh, in_specs=in_specs, out_specs=out_specs, check_vma=False)
```

profile of v0, /device:TPU:0, one launch (start us, length us, event | category | flops | bytes accessed | tf_op | source)
XLA Modules:
  0.0 769.2 jit_solution(13587244789811039244)
XLA Ops:
  12.3 3.1 fusion.33
  16.0 4.2 convolution_convert_fusion.4
  37.0 123.3 %all-reduce.8.cloned.1.call-done = bf16[2048,768]{1,0:T(8,128)(2,1)} async-done(((bf16[2048,768]{1,0:T(8,128)(2,1)}), bf16[2048,768]{1,0:T(8,128)(2,1)}) %all-reduce.8.cloned.1.call-update) | async-done | bytes 3145744 | tf_op jit(solution)/shard_map/psum | solution.py:105
  160.3 4.1 fusion.31
  166.9 18.3 %fusion.12 = (bf16[2048,768]{1,0:T(8,128)(2,1)S(1)}, f32[2048,768]{1,0:T(8,128)}) fusion(f32[768]{0:T(1024)S(1)} %convert_element_type.170, bf16[768,768]{1,0:T(8,128)(2,1)S(1)} %copy-done, f32[768]{0:T(1024)S(1)} %convert_element_type.168, f32[768]{0:T(1024)S(1)} %convert_element_type.167, f32[2048]{0:T(1024)S(1)} %add_rsqrt_fusion.1, ...), kind=kOutput, calls=%fused_computation.22 | convolution fusion | flops 2533883904 | bytes 16936960 | tf_op jit(solution)/shard_map/dot_general | solution.py:109
  186.9 4.0 convolution_convert_fusion.1
  191.0 120.1 %all-reduce.10.cloned.1.call-done = bf16[2048,768]{1,0:T(8,128)(2,1)} async-done(((bf16[2048,768]{1,0:T(8,128)(2,1)}), bf16[2048,768]{1,0:T(8,128)(2,1)}) %all-reduce.10.cloned.1.call-update) | async-done | bytes 3145744 | tf_op jit(solution)/shard_map/psum | solution.py:114
  311.2 5.4 fusion.64
  318.5 3.6 fusion.13
  322.1 3.8 fusion.8
  325.9 5.3 convert_reduce_fusion.1
  333.0 4.0 convolution_convert_fusion
  337.9 119.4 %all-reduce.12.cloned.1.call-done = bf16[2048,768]{1,0:T(8,128)(2,1)} async-done(((bf16[2048,768]{1,0:T(8,128)(2,1)}), bf16[2048,768]{1,0:T(8,128)(2,1)}) %all-reduce.12.cloned.1.call-update) | async-done | bytes 3145744 | tf_op jit(solution)/shard_map/psum | solution.py:131
  457.2 10.3 %multiply_reduce_fusion.2 = (f32[768]{0:T(1024)}, f32[2048]{0:T(1024)S(1)}, f32[2048]{0:T(1024)S(1)}, f32[768]{0:T(1024)}, f32[768]{0:T(1024)}) fusion(f32[2048,768]{1,0:T(8,128)} %copy-done.5, bf16[2048,768]{1,0:T(8,128)(2,1)} %all-reduce.12.cloned.1.call-done, f32[2048]{0:T(1024)S(1)} %add_rsqrt_fusion.1, f32[2048]{0:T(1024)S(1)} %broadcast_multiply_fusion.5, ...), kind=kLoop, calls=%fused_computation.31 | loop fusion | flops 25159424 | bytes 15776768 | tf_op jit(solution)/shard_map/reduce_sum | solution.py:48
  467.6 6.1 fusion.63
  478.1 7.8 %convert_reduce_fusion.2 = (f32[3,64]{1,0:T(4,128)}, bf16[4,3,64,512]{3,2,1,0:T(8,128)(2,1)S(1)}) fusion(f32[4,3,512,512]{2,3,1,0:T(8,128)} %copy-done.1, f32[4,3,512]{2,1,0:T(4,128)} %log_add_fusion, bf16[4,512,3,64]{1,0,3,2:T(4,128)(2,1)S(1)} %reshape.119), kind=kOutput, calls=%fused_computation.75 | convolution fusion | flops 413269824 | bytes 14181120 | tf_op jit(solution)/shard_map/bhqk,bqhd->bkhd/dot_general | solution.py:146
  485.9 9.1 %multiply_reduce_fusion = (f32[4,3,512]{2,1,0:T(4,128)S(1)}, f32[4,3,512,512]{2,3,1,0:T(8,128)}) fusion(f32[4,3,512,512]{2,3,1,0:T(8,128)} %copy-done.1, f32[4,3,512]{2,1,0:T(4,128)S(1)} %copy-done.22, bf16[4,512,3,64]{1,0,3,2:T(4,128)(2,1)S(1)} %reshape.116, bf16[4,512,3,64]{1,0,3,2:T(4,128)(2,1)S(1)} %reshape.119), kind=kOutput, calls=%fused_computation.1 | convolution fusion | flops 415229952 | bytes 26787840 | tf_op jit(solution)/shard_map/bqhd,bkhd->bhqk/dot_general | solution.py:150
  495.1 7.1 multiply_convert_fusion
  513.7 8.0 %fusion.37 = f32[768,768]{1,0:T(8,128)} fusion(bf16[2048,768]{1,0:T(8,128)(2,1)} %copy-done.18, f32[2048,768]{1,0:T(8,128)} %copy-done.5), kind=kOutput, calls=%fused_computation.82 | convolution fusion | flops 2417491968 | bytes 11796480 | tf_op jit(solution)/shard_map/dot_general | solution.py:29
  521.7 4.9 fusion.46
  533.4 26.1 %all-reduce = (f32[192]{0:T(256)}, f32[192]{0:T(256)}, f32[768]{0:T(1024)}, f32[768]{0:T(1024)}, f32[768]{0:T(1024)}, /*index=5*/f32[768]{0:T(1024)}, f32[768]{0:T(1024)}, f32[768]{0:T(1024)}, f32[768]{0:T(1024)}) all-reduce(f32[192]{0:T(256)S(1)} %reduce_sum.186, ...), channel_id=1, replica_groups=mesh['dp'=8,'tensor'=4] {'dp'}, use_global_device_ids=true, to_apply=%region_17.0 | all-reduce | flops 5760 | bytes 46080 | tf_op jit(solution)/shard_map/psum | solution.py:195
  559.5 74.1 %all-reduce.14.cloned.1.call-done = bf16[2048,768]{1,0:T(8,128)(2,1)} async-done(((bf16[2048,768]{1,0:T(8,128)(2,1)}), bf16[2048,768]{1,0:T(8,128)(2,1)}) %all-reduce.14.cloned.1.call-update) | async-done | bytes 3145744 | tf_op jit(solution)/shard_map/psum | solution.py:177
  633.6 6.1 add_convert_fusion
  639.7 112.0 %all-reduce.16.cloned.1.call-done = (f32[768,192]{0,1:T(8,128)}, f32[768,192]{0,1:T(8,128)}, f32[768,192]{0,1:T(8,128)}, f32[192,768]{1,0:T(8,128)}, f32[768,768]{1,0:T(8,128)}, /*index=5*/f32[768,768]{1,0:T(8,128)}) async-done(((f32[768,192]{0,1:T(8,128)}, f32[768,192]{0,1:T(8,128)}, f32[768,192]{0,1:T(8,128)}, f32[192,768]{1,0:T(8,128)}, f32[768,768]{1,0:T(8,128)}, /*index=5*/f32[768,768]{1,0:T(8,128)}), ...) | async-done | bytes 7077904 | tf_op jit(solution)/shard_map/psum | solution.py:195
  (185 shorter events, 64.2 us)
Async XLA Ops:
  7.2 159.6 %copy-start = (bf16[768,768]{1,0:T(8,128)(2,1)S(1)}, bf16[768,768]{1,0:T(8,128)(2,1)}, u32[]{:S(2)}) copy-start(bf16[768,768]{1,0:T(8,128)(2,1)} %param.27) | copy-start | bytes 3538948
  7.2 153.1 %all-reduce.8.cloned.1.call-start = ((), (), s32[]{:S(2)}) async-start(), calls=%async_computation | async-start | bytes 6291456 | tf_op jit(solution)/shard_map/psum | solution.py:105
  16.0 8.4 %copy-start.14 = (bf16[4,512,3,64]{1,0,3,2:T(4,128)(2,1)}, bf16[4,512,3,64]{1,0,3,2:T(4,128)(2,1)S(1)}, u32[]{:S(2)}) copy-start(bf16[4,512,3,64]{1,0,3,2:T(4,128)(2,1)S(1)} %reshape.117) | copy-start | bytes 2359300
  36.4 274.8 %all-reduce.10.cloned.1.call-start = ((), (), s32[]{:S(2)}) async-start(), calls=%async_computation.1 | async-start | bytes 6291456 | tf_op jit(solution)/shard_map/psum | solution.py:114
  37.0 274.2 %copy-start.35 = (f32[768]{0:T(1024)}, f32[768]{0:T(1024)S(1)}, u32[]{:S(2)}) copy-start(f32[768]{0:T(1024)S(1)} %convert_element_type.168) | copy-start | bytes 9220
  166.8 300.7 %copy-start.28 = (f32[2048]{0:T(1024)}, f32[2048]{0:T(1024)S(1)}, u32[]{:S(2)}) copy-start(f32[2048]{0:T(1024)S(1)} %add_rsqrt_fusion.1) | copy-start | bytes 24580
  166.8 20.1 %copy-start.48 = (bf16[768,768]{1,0:T(8,128)(2,1)S(1)}, bf16[768,768]{1,0:T(8,128)(2,1)}, u32[]{:S(2)}) copy-start(bf16[768,768]{1,0:T(8,128)(2,1)} %param.29) | copy-start | bytes 3538948
  190.9 266.3 %all-reduce.12.cloned.1.call-start = ((), (), s32[]{:S(2)}) async-start(), calls=%async_computation.2 | async-start | bytes 6291456 | tf_op jit(solution)/shard_map/psum | solution.py:131
  337.0 296.6 %all-reduce.14.cloned.1.call-start = ((), (), s32[]{:S(2)}) async-start(), calls=%async_computation.3 | async-start | bytes 6291456 | tf_op jit(solution)/shard_map/psum | solution.py:177
  457.2 10.3 %copy-start.3 = (bf16[2048,768]{1,0:T(8,128)(2,1)S(1)}, bf16[2048,768]{1,0:T(8,128)(2,1)}, u32[]{:S(2)}) copy-start(bf16[2048,768]{1,0:T(8,128)(2,1)} %param.17) | copy-start | bytes 9437188
  457.2 10.3 %copy-start.8 = (bf16[2048,768]{1,0:T(8,128)(2,1)S(1)}, bf16[2048,768]{1,0:T(8,128)(2,1)}, u32[]{:S(2)}) copy-start(bf16[2048,768]{1,0:T(8,128)(2,1)} %all-reduce.8.cloned.1.call-done) | copy-start | bytes 9437188
  457.2 10.3 %copy-start.11 = (bf16[2048,768]{1,0:T(8,128)(2,1)S(1)}, bf16[2048,768]{1,0:T(8,128)(2,1)}, u32[]{:S(2)}) copy-start(bf16[2048,768]{1,0:T(8,128)(2,1)} %all-reduce.12.cloned.1.call-done) | copy-start | bytes 9437188
  478.1 7.8 %copy-start.22 = (f32[4,3,512]{2,1,0:T(4,128)S(1)}, f32[4,3,512]{2,1,0:T(4,128)}, u32[]{:S(2)}) copy-start(f32[4,3,512]{2,1,0:T(4,128)} %log_add_fusion) | copy-start | bytes 73732
  478.1 16.9 %slice-start = ((s8[12582912]{0:T(1024)(128)(4,1)}), s8[4194304]{0:T(1024)(128)(4,1)S(1)}, s32[]{:S(2)}) async-start(s8[12582912]{0:T(1024)(128)(4,1)} %bitcast.72), calls=%async_computation.5 | async-start | bytes 8388608
  478.1 16.9 %slice-start.1 = ((s8[12582912]{0:T(1024)(128)(4,1)}), s8[4194304]{0:T(1024)(128)(4,1)S(1)}, s32[]{:S(2)}) async-start(s8[12582912]{0:T(1024)(128)(4,1)} %bitcast.72), calls=%async_computation.6 | async-start | bytes 8388608
  485.9 9.1 %slice-start.2 = ((s8[12582912]{0:T(1024)(128)(4,1)}), s8[4194304]{0:T(1024)(128)(4,1)S(1)}, s32[]{:S(2)}) async-start(s8[12582912]{0:T(1024)(128)(4,1)} %bitcast.72), calls=%async_computation.7 | async-start | bytes 8388608
  513.4 238.3 %all-reduce.16.cloned.1.call-start = ((), (), s32[]{:S(2)}) async-start(), calls=%async_computation.4 | async-start | bytes 14155776 | tf_op jit(solution)/shard_map/psum | solution.py:195
  513.7 8.0 %copy-start.4 = (bf16[2048,768]{1,0:T(8,128)(2,1)S(1)}, bf16[2048,768]{1,0:T(8,128)(2,1)}, u32[]{:S(2)}) copy-start(bf16[2048,768]{1,0:T(8,128)(2,1)} %param.17) | copy-start | bytes 9437188
  513.7 8.0 %copy-start.9 = (bf16[2048,768]{1,0:T(8,128)(2,1)S(1)}, bf16[2048,768]{1,0:T(8,128)(2,1)}, u32[]{:S(2)}) copy-start(bf16[2048,768]{1,0:T(8,128)(2,1)} %all-reduce.8.cloned.1.call-done) | copy-start | bytes 9437188
  513.7 8.0 %copy-start.29 = (f32[2048]{0:T(1024)S(1)}, f32[2048]{0:T(1024)}, u32[]{:S(2)}) copy-start(f32[2048]{0:T(1024)} %copy-done.28) | copy-start | bytes 24580
  513.7 8.0 %copy-start.36 = (f32[768]{0:T(1024)S(1)}, f32[768]{0:T(1024)}, u32[]{:S(2)}) copy-start(f32[768]{0:T(1024)} %copy-done.35) | copy-start | bytes 9220
  513.7 8.0 %copy-start.51 = (bf16[2048,768]{1,0:T(8,128)(2,1)S(1)}, bf16[2048,768]{1,0:T(8,128)(2,1)}, u32[]{:S(2)}) copy-start(bf16[2048,768]{1,0:T(8,128)(2,1)} %copy-done.50) | copy-start | bytes 9437188
  751.6 7.8 %copy-start.20 = (f32[768,768]{1,0:T(8,128)S(1)}, f32[768,768]{1,0:T(8,128)}, u32[]{:S(2)}) copy-start(f32[768,768]{1,0:T(8,128)} %get-tuple-element.72) | copy-start | bytes 7077892
  751.6 9.2 %copy-start.19 = (f32[768,768]{1,0:T(8,128)S(1)}, f32[768,768]{1,0:T(8,128)}, u32[]{:S(2)}) copy-start(f32[768,768]{1,0:T(8,128)} %get-tuple-element.74) | copy-start | bytes 7077892
  (40 other events, 131.3 us)
Sparse Core Ops, SparseCore 0:
  36.5 123.7 all-reduce.7
  191.0 120.0 all-reduce.9
  337.1 120.0 all-reduce.11
  513.5 120.0 all-reduce.13
  638.7 112.9 all-reduce.15
where the time goes:
time: 778 us; the launch traced here: 769 us
  waiting for transfers between devices  549 us (71%)
  matrix products  95.3 us (12%)
  other arithmetic  53.1 us (7%)
  local copies, waits for them, and re-layouts  29.5 us (4%)
  blocking collectives  26.1 us (3%)
  between operations  15 us (2%)
    psum x1, waiting for transfers between devices, shards(): lax.psum(attn_part.astype(jnp.bfloat16), 'tensor').astype(jnp.float32)  123 us
    psum x1, waiting for transfers between devices, shards(): lax.psum(ffn_part.astype(jnp.bfloat16), 'tensor').astype(jnp.float32)  120 us
    psum x1, waiting for transfers between devices, shards(): lax.psum(normed_part.astype(jnp.bfloat16), 'tensor').astype(jnp.float32)  119 us
    psum x1, waiting for transfers between devices, shards(): lax.psum((query_weight_grad, query_bias_grad, key_weight_grad, value_weig...  112 us
    psum x1, waiting for transfers between devices, shards(): lax.psum(input_part.astype(jnp.bfloat16), 'tensor').astype(jnp.float32)  74.1 us
    psum x1, blocking collectives, shards(): lax.psum((query_weight_grad, query_bias_grad, key_weight_grad, value_weig...  26.1 us
    unnamed x128, local copies, waits for them, and re-layouts  22.9 us
    reduce_sum x3, other arithmetic, column_total(): return jnp.sum(values, axis=0, dtype=jnp.float32)  20 us
  transfers between devices with their start and end apart: 5, of which 5 were waited for; matrix products, arithmetic and copies ran while one was open for 3% of the time, Pallas kernels for 0%

commit v1 on v0

v1 whole, which is shorter than its diff:
```python
import jax
import jax.numpy as jnp
from jax import lax
from jax.sharding import PartitionSpec as P

LEN = 512
HDIM = 64
GROUP = 8
epsilon = 1e-12
root_half = 0.7071067811865476
density_norm = 0.3989422804014327
f32 = jnp.float32
bf16 = jnp.bfloat16


def norm_parts(values):
    center = values - jnp.mean(values, axis=-1, keepdims=True)
    inverse = lax.rsqrt(jnp.mean(center * center, axis=-1, keepdims=True) + epsilon)
    return center * inverse, inverse


def norm_back(grad_out, normal, inverse, norm_gain):
    scaled = grad_out * norm_gain.astype(f32)
    first_mean = jnp.mean(scaled, axis=-1, keepdims=True)
    cross_mean = jnp.mean(scaled * normal, axis=-1, keepdims=True)
    return inverse * (scaled - first_mean - normal * cross_mean)


def dot(left, right, dims):
    return lax.dot_general(left, right, (dims, ((), ())), preferred_element_type=f32)


def gelu_slope(values):
    return (
        0.5 * (1.0 + lax.erf(values * root_half))
        + values * jnp.exp(-0.5 * values * values) * density_norm
    )


def make_shards(n_dp, n_tensor):
    def flip_dp(values, bit):
        return lax.ppermute(values, "dp", [(i, i ^ bit) for i in range(n_dp)])

    def flip_core(values):
        return flip_dp(values, 1)

    def flip_x(values):
        return flip_dp(values, 2)

    def flip_y(values):
        return flip_dp(values, 4)

    def flip_tensor(values, bit):
        return lax.ppermute(values, "tensor", [(i, i ^ bit) for i in range(n_tensor)])

    def ring(values):
        return lax.ppermute(values, "tensor", [(i, (i + 1) % n_tensor) for i in range(n_tensor)])

    def spread(own, quarter, core):
        rows = own.shape[0]
        half = rows // 16 * 8
        from_x = flip_x(own)
        from_y = flip_y(own)
        diag = jnp.concatenate([flip_x(from_y[:half]), flip_y(from_x[half:])])
        four = jnp.stack([own, from_x, from_y, diag])
        other = flip_core(four)
        four = jnp.stack([four[quarter ^ j] for j in range(4)])
        other = jnp.stack([other[quarter ^ j] for j in range(4)])
        return jnp.where(core == 0, jnp.concatenate([four, other]), jnp.concatenate([other, four]))

    def gather_rows(values, index):
        pieces = [values]
        for _ in range(n_tensor - 1):
            pieces.append(ring(pieces[-1]))
        rows = values.shape[0]
        out = jnp.zeros((n_tensor * rows, values.shape[1]), values.dtype)
        for step, piece in enumerate(pieces):
            out = lax.dynamic_update_slice(out, piece, (((index - step) % n_tensor) * rows, 0))
        return out

    def shards(
        hidden_in, query_weight, query_bias, key_weight, value_weight, value_bias,
        output_weight, output_bias, attn_gain, attn_shift, up_weight, up_bias,
        down_weight, down_bias, ffn_gain, ffn_shift, cotangent,
    ):
        width = hidden_in.shape[1]
        rows = hidden_in.shape[0] // n_tensor
        seqs = rows // LEN
        head_block = query_weight.shape[1]
        ff_block = up_weight.shape[1]
        heads = head_block // HDIM
        score_scale = HDIM ** (-0.5)
        t = lax.axis_index("tensor")
        r = lax.axis_index("dp") % GROUP
        core = r & 1
        quarter = r >> 1
        position = core * 4 + quarter

        x = lax.dynamic_slice(hidden_in, (t * rows, 0), (rows, width))
        cot = lax.dynamic_slice(cotangent, (t * rows, 0), (rows, width))
        slice_rows = 4 * head_block // GROUP
        ff_slice = ff_block // GROUP

        pack_attn = jnp.concatenate([query_weight.T, key_weight.T, value_weight.T, output_weight])
        pack_up = up_weight.T
        pack_down = down_weight

        def take(pack, size):
            return lax.dynamic_slice(pack, (position * size, 0), (size, width))

        bias_rows = jnp.zeros((8, width), bf16)
        bias_rows = bias_rows.at[0, :ff_block].set(up_bias)
        bias_rows = bias_rows.at[1, :head_block].set(query_bias)
        bias_rows = bias_rows.at[2, :head_block].set(value_bias)

        def gather_pack(pack, size, extra=None):
            own = take(pack, size)
            sent = own if extra is None else jnp.concatenate([own, extra])
            got = [flip_tensor(sent, k) for k in range(1, n_tensor)]
            z = jnp.concatenate([g[:size] for g in got])
            full = spread(z, quarter, core)
            full = full.reshape(GROUP, n_tensor - 1, size, width).transpose(1, 0, 2, 3)
            full = full.reshape(n_tensor - 1, GROUP * size, width)
            full = jnp.concatenate([pack[None], full])
            return full, [g[size:] for g in got]

        attn_all, extras = gather_pack(pack_attn, slice_rows, bias_rows)
        up_all, _ = gather_pack(pack_up, ff_slice)
        down_all, _ = gather_pack(pack_down, ff_slice)
        biases = jnp.stack([bias_rows] + extras)
        wq, wk, wv, wo = [
            attn_all[:, i * head_block : (i + 1) * head_block].reshape(n_tensor * head_block, width)
            for i in range(4)
        ]
        wu = up_all.reshape(n_tensor * ff_block, width)
        wd = down_all.reshape(n_tensor * ff_block, width)
        up_b = biases[:, 0, :ff_block].reshape(-1).astype(f32)
        query_b = biases[:, 1, :head_block].reshape(-1).astype(f32)
        value_b = biases[:, 2, :head_block].reshape(-1).astype(f32)

        nt = ((1,), (1,))
        nn = ((1,), (0,))
        tn = ((0,), (0,))
        all_heads = n_tensor * heads
        head_shape = (seqs, LEN, all_heads, HDIM)
        inputs = x.astype(f32)
        queries = (dot(x, wq, nt) + query_b).astype(bf16)
        keys = dot(x, wk, nt).astype(bf16)
        values = (dot(x, wv, nt) + value_b).astype(bf16)
        qh, kh, vh = (v.reshape(head_shape) for v in (queries, keys, values))
        scores = jnp.einsum("bqhd,bkhd->bhqk", qh, kh, preferred_element_type=f32) * score_scale
        peak = jnp.max(scores, axis=-1, keepdims=True)
        exp_scores = jnp.exp(scores - peak)
        total = jnp.sum(exp_scores, axis=-1, keepdims=True)
        probs = (exp_scores / total).astype(bf16)
        log_total = peak + jnp.log(total)
        mixed = jnp.einsum("bhqk,bkhd->bqhd", probs, vh, preferred_element_type=f32)
        mixed = mixed.reshape(rows, n_tensor * head_block).astype(bf16)
        attn = dot(mixed, wo, nn)
        hat1, inv1 = norm_parts(inputs + attn + output_bias.astype(f32))
        first = hat1 * attn_gain.astype(f32) + attn_shift.astype(f32)
        first_low = first.astype(bf16)
        pre = dot(first_low, wu, nt) + up_b
        active = jax.nn.gelu(pre, approximate=False).astype(bf16)
        ffn = dot(active, wd, nn)
        hat2, inv2 = norm_parts(first + ffn + down_bias.astype(f32))
        out_rows = (hat2 * ffn_gain.astype(f32) + ffn_shift.astype(f32)).astype(bf16)
        layer_out = gather_rows(out_rows, t)

        grad_out = cot.astype(f32)
        sums = {}
        sums["ffn_gain"] = jnp.sum(grad_out * hat2, axis=0)
        sums["ffn_shift"] = jnp.sum(grad_out, axis=0)
        grad_second = norm_back(grad_out, hat2, inv2, ffn_gain)
        sums["down_bias"] = jnp.sum(grad_second, axis=0)
        second_low = grad_second.astype(bf16)
        grad_pre = (dot(second_low, wd, nt) * gelu_slope(pre)).astype(bf16)
        sums["up_bias"] = jnp.sum(grad_pre, axis=0, dtype=f32)
        grad_first = grad_second + dot(grad_pre, wu, nn)
        sums["attn_gain"] = jnp.sum(grad_first * hat1, axis=0)
        sums["attn_shift"] = jnp.sum(grad_first, axis=0)
        grad_resid = norm_back(grad_first, hat1, inv1, attn_gain)
        sums["output_bias"] = jnp.sum(grad_resid, axis=0)
        resid_low = grad_resid.astype(bf16)
        grad_context = dot(resid_low, wo, nt).astype(bf16).reshape(head_shape)
        scores_again = jnp.einsum("bqhd,bkhd->bhqk", qh, kh, preferred_element_type=f32) * score_scale
        probs_full = jnp.exp(scores_again - log_total)
        probs_low = probs_full.astype(bf16)
        value_grad = jnp.einsum("bhqk,bqhd->bkhd", probs_low, grad_context, preferred_element_type=f32)
        value_grad = value_grad.reshape(rows, -1).astype(bf16)
        grad_probs = jnp.einsum("bqhd,bkhd->bhqk", grad_context, vh, preferred_element_type=f32)
        inner = jnp.sum(probs_full * grad_probs, axis=-1, keepdims=True)
        grad_scores = (probs_full * (grad_probs - inner)).astype(bf16)
        query_grad = jnp.einsum("bhqk,bkhd->bqhd", grad_scores, kh, preferred_element_type=f32)
        query_grad = (query_grad * score_scale).reshape(rows, -1).astype(bf16)
        key_grad = jnp.einsum("bhqk,bqhd->bkhd", grad_scores, qh, preferred_element_type=f32)
        key_grad = (key_grad * score_scale).reshape(rows, -1).astype(bf16)
        sums["query_bias"] = jnp.sum(query_grad, axis=0, dtype=f32)
        sums["value_bias"] = jnp.sum(value_grad, axis=0, dtype=f32)
        input_rows = (
            grad_resid + dot(query_grad, wq, nn) + dot(key_grad, wk, nn) + dot(value_grad, wv, nn)
        ).astype(bf16)
        input_grad = gather_rows(input_rows, t)

        def half(left, block):
            v = left.reshape(rows, n_tensor, 2, block // 2)
            mine = lax.dynamic_index_in_dim(v, core, 2, keepdims=False).reshape(rows, -1)
            sent = lax.dynamic_index_in_dim(v, 1 - core, 2, keepdims=False).reshape(rows, -1)
            return jnp.concatenate([mine, flip_core(sent)])

        def both(right):
            return jnp.concatenate([right, flip_core(right)])

        def scatter(grad, size):
            g = grad.astype(bf16).reshape(n_tensor, 2, 2, size, width)
            xb, yb = quarter & 1, quarter >> 1
            lo, hi = g[: n_tensor // 2], g[n_tensor // 2 :]

            def pick(v, axis, index):
                return lax.dynamic_index_in_dim(v, index, axis, keepdims=False)

            lo = pick(lo, 2, xb).astype(f32) + flip_x(pick(lo, 2, 1 - xb)).astype(f32)
            hi = pick(hi, 1, yb).astype(f32) + flip_y(pick(hi, 1, 1 - yb)).astype(f32)
            lo = lo.astype(bf16)
            hi = hi.astype(bf16)
            lo = pick(lo, 1, yb).astype(f32) + flip_y(pick(lo, 1, 1 - yb)).astype(f32)
            hi = pick(hi, 1, xb).astype(f32) + flip_x(pick(hi, 1, 1 - xb)).astype(f32)
            mine = jnp.concatenate([lo, hi])
            low = mine.astype(bf16)
            total = mine[0]
            for k in range(1, n_tensor):
                total = total + flip_tensor(low[k], k).astype(f32)
            return total

        def weight_grad(left, right, block):
            return dot(half(left, block), both(right), tn).reshape(n_tensor, block // 2, width)

        down_slice = scatter(weight_grad(active, second_low, ff_block), ff_slice)
        up_slice = scatter(weight_grad(grad_pre, first_low, ff_block), ff_slice)
        attn_left = jnp.stack(
            [v.reshape(rows, n_tensor, head_block) for v in (query_grad, key_grad, value_grad, mixed)], axis=2
        )
        first_half = attn_left[:, :, :2].reshape(rows, -1)
        last_half = attn_left[:, :, 2:].reshape(rows, -1)
        mine = jnp.where(core == 0, first_half, last_half)
        sent = jnp.where(core == 0, last_half, first_half)
        left = jnp.concatenate([mine, flip_core(sent)])
        xs = both(x)
        rs = both(resid_low)
        left = left.reshape(2 * rows, n_tensor, 2, head_block)
        p0 = dot(left[:, :, 0].reshape(2 * rows, -1), xs, tn).reshape(n_tensor, head_block, width)
        right = jnp.where(core == 0, xs, rs)
        p1 = dot(left[:, :, 1].reshape(2 * rows, -1), right, tn).reshape(n_tensor, head_block, width)
        attn_slice = scatter(jnp.concatenate([p0, p1], axis=1), slice_rows)
        slices = jnp.concatenate([down_slice, up_slice, attn_slice])

        def blocks(values, block):
            v = values.reshape(n_tensor, block)
            v = jnp.where((t & 1) == 1, v.reshape(n_tensor // 2, 2, block)[:, ::-1].reshape(v.shape), v)
            return jnp.where((t & 2) == 2, jnp.concatenate([v[2:], v[:2]]), v)

        small = jnp.concatenate([
            blocks(sums["up_bias"], ff_block).reshape(-1),
            blocks(sums["query_bias"], head_block).reshape(-1),
            blocks(sums["value_bias"], head_block).reshape(-1),
            sums["output_bias"], sums["attn_gain"], sums["attn_shift"],
            sums["down_bias"], sums["ffn_gain"], sums["ffn_shift"],
        ])
        small = small.reshape(-1, width)
        for bit in (1, 2, 4):
            small = small + flip_dp(small, bit)
        for bit in (1, 2):
            small = small + flip_tensor(small, bit)
        if n_dp > GROUP:
            groups = [[g * GROUP + i for g in range(n_dp // GROUP)] for i in range(GROUP)]
            slices = lax.psum(slices, "dp", axis_index_groups=groups)
            small = lax.psum(small, "dp", axis_index_groups=groups)
        full = spread(slices.astype(bf16), quarter, core).astype(f32)
        down_grad = full[:, :ff_slice].reshape(ff_block, width)
        up_grad = full[:, ff_slice : 2 * ff_slice].reshape(ff_block, width).T
        attn_grad = full[:, 2 * ff_slice :].reshape(4 * head_block, width)
        small = small.reshape(-1)
        pos = [0]

        def part(count):
            v = small[pos[0] : pos[0] + count]
            pos[0] += count
            return v

        def own(count, block):
            v = part(count).reshape(n_tensor, block)
            return lax.dynamic_index_in_dim(v, t, 0, keepdims=False)

        up_bias_grad = own(n_tensor * ff_block, ff_block)
        query_bias_grad = own(n_tensor * head_block, head_block)
        value_bias_grad = own(n_tensor * head_block, head_block)
        (output_bias_grad, attn_gain_grad, attn_shift_grad, down_bias_grad, ffn_gain_grad, ffn_shift_grad) = [
            part(width) for _ in range(6)
        ]
        return (
            layer_out, input_grad,
            attn_grad[:head_block].T, query_bias_grad,
            attn_grad[head_block : 2 * head_block].T,
            attn_grad[2 * head_block : 3 * head_block].T, value_bias_grad,
            attn_grad[3 * head_block :], output_bias_grad, attn_gain_grad, attn_shift_grad,
            up_grad, up_bias_grad, down_grad, down_bias_grad, ffn_gain_grad, ffn_shift_grad,
        )

    return shards


def solution(mesh):
    in_specs = (
        P("dp", None), P(None, "tensor"), P("tensor"), P(None, "tensor"), P(None, "tensor"), P("tensor"),
        P("tensor", None), P(), P(), P(), P(None, "tensor"), P("tensor"), P("tensor", None), P(), P(), P(),
        P("dp", None),
    )
    out_specs = (
        P("dp", None), P("dp", None), P(None, "tensor"), P("tensor"), P(None, "tensor"), P(None, "tensor"),
        P("tensor"), P("tensor", None), P(), P(), P(), P(None, "tensor"), P("tensor"), P("tensor", None),
        P(), P(), P(),
    )
    shards = make_shards(mesh.shape["dp"], mesh.shape["tensor"])
    return jax.shard_map(shards, mesh=mesh, in_specs=in_specs, out_specs=out_specs, check_vma=False)
```

time: 778 us -> 519 us (0.67)
  waiting for transfers between devices: 549 us -> 124 us
  local copies, waits for them, and re-layouts: 29.5 us -> 141 us
  starting transfers between devices: 1.09 us -> 92.9 us
  blocking collectives: 26.1 us -> 0 us
  between operations: 15 us -> 2.77 us
  matrix products: 95.3 us -> 107 us
  other arithmetic: 53.1 us -> 42.6 us
    psum x5 -> x0, waiting for transfers between devices: 549 us -> none  [the longest x1 123 us: shards(): lax.psum(attn_part.astype(jnp.bfloat16), 'tensor').astype(jnp.float32)]
    ppermute x0 -> x68, waiting for transfers between devices: none -> 124 us  [the longest x42 71.3 us: flip_dp(): return lax.ppermute(values, 'dp', [(i, i ^ bit) for i in range(n_dp)])]
    ppermute x0 -> x68, starting transfers between devices: none -> 92.9 us  [the longest x20 50 us: flip_tensor(): lax.ppermute(values, 'tensor', [(i, i ^ bit) for i in range(n_tensor)])]
    unnamed x128 -> x175, local copies, waits for them, and re-layouts: 22.9 us -> 60.6 us
    dynamic_slice x0 -> x26, local copies, waits for them, and re-layouts: none -> 29.1 us  [the longest x2 18.4 us: half(): lax.dynamic_index_in_dim(v, core, 2, keepdims=False).reshape(rows, -1)]
    reduce_sum x6 -> x4, other arithmetic: 31.5 us -> 3.93 us  [the longest x1 2.09 us: shards(): total = jnp.sum(exp_scores, axis=-1, keepdims=True)]
    psum x1 -> x0, blocking collectives: 26.1 us -> none  [shards(): lax.psum((query_weight_grad, query_bias_grad, key_weight_grad, value_weig...]
    reshape x4 -> x14, local copies, waits for them, and re-layouts: 4 us -> 16 us  [the longest x2 15.5 us: half(): v = left.reshape(rows, n_tensor, 2, block // 2)]
  transfers between devices with their start and end apart: 5 -> 68, of which waited for: 5 -> 30; matrix products, arithmetic and copies ran while one was open for 3% -> 51% of each run, Pallas kernels for 0% -> 0%
where the time goes in v1:
time: 519 us; the launch traced here: 510 us
  local copies, waits for them, and re-layouts  141 us (27%)
  waiting for transfers between devices  124 us (24%)
  matrix products  107 us (21%)
  starting transfers between devices  92.9 us (18%)
  other arithmetic  42.6 us (8%)
    dot_general x16, matrix products, dot(): lax.dot_general(left, right, (dims, ((), ())), preferred_element_type=f32)  73.8 us
    ppermute x42, waiting for transfers between devices, flip_dp(): return lax.ppermute(values, 'dp', [(i, i ^ bit) for i in range(n_dp)])  71.3 us
    unnamed x175, local copies, waits for them, and re-layouts  60.6 us
    ppermute x20, starting transfers between devices, flip_tensor(): lax.ppermute(values, 'tensor', [(i, i ^ bit) for i in range(n_tensor)])  50 us
    ppermute x42, starting transfers between devices, flip_dp(): return lax.ppermute(values, 'dp', [(i, i ^ bit) for i in range(n_dp)])  34.4 us
    ppermute x20, waiting for transfers between devices, flip_tensor(): lax.ppermute(values, 'tensor', [(i, i ^ bit) for i in range(n_tensor)])  33.3 us
    ppermute x6, waiting for transfers between devices, ring(): lax.ppermute(values, 'tensor', [(i, (i + 1) % n_tensor) for i in range(n_...  19.5 us
    dynamic_slice x2, local copies, waits for them, and re-layouts, half(): lax.dynamic_index_in_dim(v, core, 2, keepdims=False).reshape(rows, -1)  18.4 us
  transfers between devices with their start and end apart: 68, of which 30 were waited for; matrix products, arithmetic and copies ran while one was open for 51% of the time, Pallas kernels for 0%

profile of v1, /device:TPU:0, one launch (start us, length us, event | category | flops | bytes accessed | tf_op | source)
XLA Modules:
  0.0 509.7 jit_solution(3498554006426733478)
XLA Ops:
  26.4 7.6 %collective-permute-done.17 = bf16[96,768]{1,0:T(8,128)(2,1)S(1)} collective-permute-done((bf16[96,768]{1,0:T(8,128)(2,1)S(1)}, bf16[96,768]{1,0:T(8,128)(2,1)S(1)}, u32[]{:S(2)}, u32[]{:S(2)}) %collective-permute-start.17) | collective-permute-done | bytes 147488 | tf_op jit(solution)/shard_map/ppermute | solution.py:54
  72.5 9.1 %collective-permute-done.4 = bf16[288,768]{1,0:T(8,128)(2,1)S(1)} collective-permute-done((bf16[288,768]{1,0:T(8,128)(2,1)S(1)}, bf16[288,768]{1,0:T(8,128)(2,1)S(1)}, u32[]{:S(2)}, u32[]{:S(2)}) %collective-permute-start.4) | collective-permute-done | bytes 442400 | tf_op jit(solution)/shard_map/ppermute | solution.py:42
  132.3 19.0 %fusion.6 = (bf16[512,3072]{1,0:T(8,128)(2,1)}, f32[512,3072]{1,0:T(8,128)}) fusion(f32[3072]{0:T(1024)S(1)} %bitcast.472, bf16[512,768]{1,0:T(8,128)(2,1)} %fusion.60, bf16[3072,768]{1,0:T(8,128)(2,1)S(1)} %bitcast.385), kind=kOutput, calls=%fused_computation.16 | convolution fusion | flops 2519728128 | bytes 14954496 | tf_op jit(solution)/shard_map/dot_general | solution.py:30
  151.3 7.1 %reshape.628 = bf16[512,4,2,384]{3,2,1,0:T(2,128)(2,1)S(1)} reshape(bf16[512,3072]{1,0:T(8,128)(2,1)} %get-tuple-element.204) | data formatting | bytes 6291456 | tf_op jit(solution)/shard_map/reshape | solution.py:206
  169.8 7.5 %convert_reduce_fusion = (f32[3072]{0:T(1024)S(1)}, bf16[512,3072]{1,0:T(8,128)(2,1)}) fusion(f32[512,3072]{1,0:T(8,128)S(1)} %copy-done.57, f32[3072]{0:T(1024)S(1)} %bitcast.473, bf16[512,768]{1,0:T(8,128)(2,1)} %convert_element_type.411, bf16[3072,768]{1,0:T(8,128)(2,1)} %bitcast.387), kind=kOutput, calls=%fused_computation.23 | convolution fusion | flops 2436363264 | bytes 14966784 | tf_op jit(solution)/shard_map/dot_general | solution.py:30
  177.3 8.4 %reshape.631 = bf16[512,4,2,384]{3,2,1,0:T(2,128)(2,1)} reshape(bf16[512,3072]{1,0:T(8,128)(2,1)} %get-tuple-element.214) | data formatting | bytes 6291456 | tf_op jit(solution)/shard_map/reshape | solution.py:206
  185.8 7.3 %multiply_reduce_fusion.2 = (f32[768]{0:T(1024)S(1)}, f32[512]{0:T(512)S(1)}, f32[512]{0:T(512)S(1)}, f32[768]{0:T(1024)S(1)}, f32[512,768]{1,0:T(8,128)S(1)}) fusion(f32[512,768]{1,0:T(8,128)} %copy-done.9, f32[512]{0:T(512)S(1)} %add_rsqrt_fusion.1, f32[512]{0:T(512)S(1)} %broadcast_multiply_fusion.5, f32[768]{0:T(1024)S(1)} %convert_element_type.400, ...), kind=kOutput, calls=%fused_computation.94 | convolution fusion | flops 2419848704 | bytes 12600320 | tf_op jit(solution)/shard_map/dot_general | solution.py:30
  199.7 13.0 %multiply_reduce_fusion = (f32[12,512]{1,0:T(8,128)S(1)}, f32[12,512,512]{1,2,0:T(8,128)}) fusion(f32[12,512,512]{1,2,0:T(8,128)} %copy-done.2, f32[12,512]{1,0:T(8,128)S(1)} %log_add_fusion, bf16[512,12,64]{0,2,1:T(8,128)(2,1)} %bitcast.370, bf16[512,12,64]{0,2,1:T(8,128)(2,1)} %bitcast.419), kind=kOutput, calls=%fused_computation.1 | convolution fusion | flops 415229952 | bytes 26787840 | tf_op jit(solution)/shard_map/bqhd,bkhd->bhqk/dot_general | solution.py:191
  212.7 7.8 %convert_reduce_fusion.2 = (f32[12,64]{1,0:T(8,128)S(1)}, bf16[12,64,512]{2,1,0:T(8,128)(2,1)}) fusion(bf16[512,12,64]{0,2,1:T(8,128)(2,1)S(1)} %bitcast.371, f32[12,512,512]{1,2,0:T(8,128)} %copy-done.2, f32[12,512]{1,0:T(8,128)S(1)} %log_add_fusion), kind=kOutput, calls=%fused_computation.95 | convolution fusion | flops 413269248 | bytes 14183424 | tf_op jit(solution)/shard_map/bhqk,bqhd->bkhd/dot_general | solution.py:189
  220.7 9.9 %multiply_convert_fusion = bf16[12,512,512]{1,2,0:T(8,128)(2,1)S(1)} fusion(f32[12,512,512]{1,2,0:T(8,128)} %get-tuple-element.210, f32[12,512,512]{1,2,0:T(8,128)} %copy-done.2, f32[12,512]{1,0:T(8,128)S(1)} %get-tuple-element.209, f32[12,512]{1,0:T(8,128)S(1)} %log_add_fusion), kind=kLoop, calls=%fused_computation | loop fusion | flops 15728640 | bytes 31506432 | tf_op jit(solution)/shard_map/convert_element_type | solution.py:193
  233.7 9.2 %constant_dynamic-slice_fusion.18 = (bf16[512,4,1,384]{3,2,1,0:T(2,128)(2,1)}, bf16[512,4,1,384]{3,2,1,0:T(2,128)(2,1)}) fusion(bf16[512,4,2,384]{3,2,1,0:T(2,128)(2,1)S(1)} %reshape.628, s32[]{:T(128)S(6)} %select_n.270, s32[]{:T(128)S(6)} %select_n.271), kind=kLoop, calls=%fused_computation.295 | loop fusion | bytes 6291464 | tf_op jit(solution)/shard_map/jit(dynamic_index_in_dim)/dynamic_slice | solution.py:207
  242.9 8.7 %copy.110 = bf16[512,4,1,384]{0,3,1,2:T(8,128)(2,1)} copy(bf16[512,4,1,384]{3,2,1,0:T(2,128)(2,1)} %get-tuple-element.105) | data formatting | bytes 3145728
  251.7 9.2 %constant_dynamic-slice_fusion.12 = (bf16[512,4,1,384]{3,2,1,0:T(2,128)(2,1)}, bf16[512,4,1,384]{3,2,1,0:T(2,128)(2,1)}) fusion(bf16[512,4,2,384]{3,2,1,0:T(2,128)(2,1)S(1)} %copy-done.4, s32[]{:T(128)S(6)} %select_n.270, s32[]{:T(128)S(6)} %select_n.271), kind=kLoop, calls=%fused_computation.289 | loop fusion | bytes 6291464 | tf_op jit(solution)/shard_map/jit(dynamic_index_in_dim)/dynamic_slice | solution.py:207
  260.9 8.2 %copy.114 = bf16[512,4,1,384]{0,3,1,2:T(8,128)(2,1)} copy(bf16[512,4,1,384]{3,2,1,0:T(2,128)(2,1)} %get-tuple-element.107) | data formatting | bytes 3145728
  291.1 8.3 %copy.113 = bf16[512,4,1,384]{0,3,1,2:T(8,128)(2,1)} copy(bf16[512,4,1,384]{3,2,1,0:T(2,128)(2,1)} %get-tuple-element.106) | data formatting | bytes 3145728
  327.5 6.9 %collective-permute-done.35 = bf16[2,2,96,768]{3,2,0,1:T(8,128)(2,1)S(1)} collective-permute-done((bf16[2,2,96,768]{3,2,0,1:T(8,128)(2,1)S(1)}, bf16[2,2,96,768]{3,2,0,1:T(8,128)(2,1)S(1)}, u32[]{:S(2)}, u32[]{:S(2)}) %collective-permute-start.35) | collective-permute-done | bytes 589856 | tf_op jit(solution)/shard_map/ppermute | solution.py:42
  336.5 10.6 %collective-permute-done.44 = bf16[2,2,96,768]{3,2,0,1:T(8,128)(2,1)S(1)} collective-permute-done((bf16[2,2,96,768]{3,2,0,1:T(8,128)(2,1)S(1)}, bf16[2,2,96,768]{3,2,0,1:T(8,128)(2,1)S(1)}, u32[]{:S(2)}, u32[]{:S(2)}) %collective-permute-start.44) | collective-permute-done | bytes 589856 | tf_op jit(solution)/shard_map/ppermute | solution.py:42
  349.5 8.7 %collective-permute-done.54 = bf16[2,2,96,768]{3,2,0,1:T(8,128)(2,1)S(1)} collective-permute-done((bf16[2,2,96,768]{3,2,0,1:T(8,128)(2,1)S(1)}, bf16[2,2,96,768]{3,2,0,1:T(8,128)(2,1)S(1)}, u32[]{:S(2)}, u32[]{:S(2)}) %collective-permute-start.54) | collective-permute-done | bytes 589856 | tf_op jit(solution)/shard_map/ppermute | solution.py:42
  384.1 7.3 %collective-permute-done.37 = bf16[96,768]{1,0:T(8,128)(2,1)S(1)} collective-permute-done((bf16[96,768]{1,0:T(8,128)(2,1)S(1)}, bf16[96,768]{1,0:T(8,128)(2,1)S(1)}, u32[]{:S(2)}, u32[]{:S(2)}) %collective-permute-start.37) | collective-permute-done | bytes 147488 | tf_op jit(solution)/shard_map/ppermute | solution.py:54
  395.2 9.1 %collective-permute-start.43 = (bf16[96,768]{1,0:T(8,128)(2,1)S(1)}, bf16[96,768]{1,0:T(8,128)(2,1)S(1)}, u32[]{:S(2)}, u32[]{:S(2)}) collective-permute-start(bf16[96,768]{1,0:T(8,128)(2,1)S(1)} %fusion.87), channel_id=1, source_target_pairs={{0,1},{1,0},{2,3},{3,2},{4,5},{5,4},{6,7},{7,6},{8,9},{9,8},{10,11... | collective-permute-start | bytes 442376 | tf_op jit(solution)/shard_map/ppermute | solution.py:54
  418.3 8.0 %collective-permute-done.59 = bf16[288,768]{1,0:T(8,128)(2,1)S(1)} collective-permute-done((bf16[288,768]{1,0:T(8,128)(2,1)S(1)}, bf16[288,768]{1,0:T(8,128)(2,1)S(1)}, u32[]{:S(2)}, u32[]{:S(2)}) %collective-permute-start.59) | collective-permute-done | bytes 442400 | tf_op jit(solution)/shard_map/ppermute | solution.py:42
  446.8 6.9 %collective-permute-done.66 = f32[12,768]{1,0:T(8,128)S(1)} collective-permute-done((f32[12,768]{1,0:T(8,128)S(1)}, f32[12,768]{1,0:T(8,128)S(1)}, u32[]{:S(2)}, u32[]{:S(2)}) %collective-permute-start.66) | collective-permute-done | bytes 36896 | tf_op jit(solution)/shard_map/ppermute | solution.py:54
  473.4 9.6 %collective-permute-done.29 = bf16[512,768]{1,0:T(8,128)(2,1)} collective-permute-done((bf16[512,768]{1,0:T(8,128)(2,1)S(1)}, bf16[512,768]{1,0:T(8,128)(2,1)}, u32[]{:S(2)}, u32[]{:S(2)}) %collective-permute-start.29) | collective-permute-done | bytes 786464 | tf_op jit(solution)/shard_map/ppermute | solution.py:57
  485.1 9.9 %collective-permute-done.26 = bf16[512,768]{1,0:T(8,128)(2,1)} collective-permute-done((bf16[512,768]{1,0:T(8,128)(2,1)}, bf16[512,768]{1,0:T(8,128)(2,1)}, u32[]{:S(2)}, u32[]{:S(2)}) %collective-permute-start.26) | collective-permute-done | bytes 786464 | tf_op jit(solution)/shard_map/ppermute | solution.py:57
  (506 shorter events, 289.7 us)
Async XLA Ops:
  11.8 22.2 %collective-permute-start.17 = (bf16[96,768]{1,0:T(8,128)(2,1)S(1)}, bf16[96,768]{1,0:T(8,128)(2,1)S(1)}, u32[]{:S(2)}, u32[]{:S(2)}) collective-permute-start(bf16[96,768]{1,0:T(8,128)(2,1)S(1)} %constant_dynamic-slice_fusion.27), channel_id=1, source_target_pairs={{0,2},{1,3},{2,0},{3,1},{4,6},{5,7},{6,4},{7,5},{8,10},{9,11},{10,... | collective-permute-start | bytes 442376 | tf_op jit(solution)/shard_map/ppermute | solution.py:54
  15.2 19.4 %collective-permute-start.18 = (bf16[96,768]{1,0:T(8,128)(2,1)S(1)}, bf16[96,768]{1,0:T(8,128)(2,1)S(1)}, u32[]{:S(2)}, u32[]{:S(2)}) collective-permute-start(bf16[96,768]{1,0:T(8,128)(2,1)S(1)} %constant_dynamic-slice_fusion.27), channel_id=1, source_target_pairs={{0,3},{1,2},{2,1},{3,0},{4,7},{5,6},{6,5},{7,4},{8,11},{9,10},{10,... | collective-permute-start | bytes 442376 | tf_op jit(solution)/shard_map/ppermute | solution.py:54
  22.7 18.5 %collective-permute-start.12 = (bf16[288,768]{1,0:T(8,128)(2,1)}, bf16[288,768]{1,0:T(8,128)(2,1)}, u32[]{:S(2)}, u32[]{:S(2)}) collective-permute-start(bf16[288,768]{1,0:T(8,128)(2,1)} %constant_dynamic-update-slice_fusion.16), channel_id=1, source_target_pairs={{0,16},{4,20},{8,24},{12,28},{16,0},{20,4},{24,8},{28,12},{1,17},{... | collective-permute-start | bytes 1327112 | tf_op jit(solution)/shard_map/ppermute | solution.py:42
  24.2 19.1 %collective-permute-start.11 = (bf16[288,768]{1,0:T(8,128)(2,1)}, bf16[288,768]{1,0:T(8,128)(2,1)}, u32[]{:S(2)}, u32[]{:S(2)}) collective-permute-start(bf16[288,768]{1,0:T(8,128)(2,1)} %constant_dynamic-update-slice_fusion.16), channel_id=1, source_target_pairs={{0,8},{4,12},{8,0},{12,4},{16,24},{20,28},{24,16},{28,20},{1,9},{5... | collective-permute-start | bytes 1327112 | tf_op jit(solution)/shard_map/ppermute | solution.py:42
  36.8 18.9 %collective-permute-start.19 = (bf16[288,768]{1,0:T(8,128)(2,1)}, bf16[288,768]{1,0:T(8,128)(2,1)}, u32[]{:S(2)}, u32[]{:S(2)}) collective-permute-start(bf16[288,768]{1,0:T(8,128)(2,1)} %constant_dynamic-update-slice_fusion.35), channel_id=1, source_target_pairs={{0,8},{4,12},{8,0},{12,4},{16,24},{20,28},{24,16},{28,20},{1,9},{5... | collective-permute-start | bytes 1327112 | tf_op jit(solution)/shard_map/ppermute | solution.py:42
  46.2 21.7 %collective-permute-start = (bf16[104,768]{1,0:T(8,128)(2,1)}, bf16[104,768]{1,0:T(8,128)(2,1)}, u32[]{:S(2)}, u32[]{:S(2)}) collective-permute-start(bf16[104,768]{1,0:T(8,128)(2,1)} %pad_maximum_fusion.17), channel_id=1, source_target_pairs={{0,1},{1,0},{2,3},{3,2},{4,5},{5,4},{6,7},{7,6},{8,9},{9,8},{10,11... | collective-permute-start | bytes 479240 | tf_op jit(solution)/shard_map/ppermute | solution.py:54
  50.9 18.4 %collective-permute-start.1 = (bf16[104,768]{1,0:T(8,128)(2,1)}, bf16[104,768]{1,0:T(8,128)(2,1)S(1)}, u32[]{:S(2)}, u32[]{:S(2)}) collective-permute-start(bf16[104,768]{1,0:T(8,128)(2,1)} %pad_maximum_fusion.17), channel_id=1, source_target_pairs={{0,2},{1,3},{2,0},{3,1},{4,6},{5,7},{6,4},{7,5},{8,10},{9,11},{10,... | collective-permute-start | bytes 479240 | tf_op jit(solution)/shard_map/ppermute | solution.py:54
  63.7 27.3 %collective-permute-start.15 = (bf16[4,288,768]{2,1,0:T(8,128)(2,1)}, bf16[4,288,768]{2,1,0:T(8,128)(2,1)}, u32[]{:S(2)}, u32[]{:S(2)}) collective-permute-start(bf16[4,288,768]{2,1,0:T(8,128)(2,1)} %pad_maximum_fusion.4), channel_id=1, source_target_pairs={{0,4},{4,0},{8,12},{12,8},{16,20},{20,16},{24,28},{28,24},{1,5},{5... | collective-permute-start | bytes 5308424 | tf_op jit(solution)/shard_map/ppermute | solution.py:42
  67.0 24.0 %collective-permute-start.23 = (bf16[4,288,768]{2,1,0:T(8,128)(2,1)}, bf16[4,288,768]{2,1,0:T(8,128)(2,1)}, u32[]{:S(2)}, u32[]{:S(2)}) collective-permute-start(bf16[4,288,768]{2,1,0:T(8,128)(2,1)} %pad_maximum_fusion.5), channel_id=1, source_target_pairs={{0,4},{4,0},{8,12},{12,8},{16,20},{20,16},{24,28},{28,24},{1,5},{5... | collective-permute-start | bytes 5308424 | tf_op jit(solution)/shard_map/ppermute | solution.py:42
  67.9 251.2 %collective-permute-start.49 = (bf16[512,768]{1,0:T(8,128)(2,1)}, bf16[512,768]{1,0:T(8,128)(2,1)}, u32[]{:S(2)}, u32[]{:S(2)}) collective-permute-start(bf16[512,768]{1,0:T(8,128)(2,1)} %constant_dynamic-slice_fusion.45), channel_id=1, source_target_pairs={{0,4},{4,0},{8,12},{12,8},{16,20},{20,16},{24,28},{28,24},{1,5},{5... | collective-permute-start | bytes 2359304 | tf_op jit(solution)/shard_map/ppermute | solution.py:42
  131.8 178.6 %collective-permute-start.40 = (bf16[512,768]{1,0:T(8,128)(2,1)}, bf16[512,768]{1,0:T(8,128)(2,1)}, u32[]{:S(2)}, u32[]{:S(2)}) collective-permute-start(bf16[512,768]{1,0:T(8,128)(2,1)} %fusion.60), channel_id=1, source_target_pairs={{0,4},{4,0},{8,12},{12,8},{16,20},{20,16},{24,28},{28,24},{1,5},{5... | collective-permute-start | bytes 2359304 | tf_op jit(solution)/shard_map/ppermute | solution.py:42
  168.8 136.2 %collective-permute-start.31 = (bf16[512,768]{1,0:T(8,128)(2,1)}, bf16[512,768]{1,0:T(8,128)(2,1)}, u32[]{:S(2)}, u32[]{:S(2)}) collective-permute-start(bf16[512,768]{1,0:T(8,128)(2,1)} %convert_element_type.411), channel_id=1, source_target_pairs={{0,4},{4,0},{8,12},{12,8},{16,20},{20,16},{24,28},{28,24},{1,5},{5... | collective-permute-start | bytes 2359304 | tf_op jit(solution)/shard_map/ppermute | solution.py:42
  251.6 53.4 %collective-permute-start.30 = (bf16[512,1536]{0,1:T(8,128)(2,1)}, bf16[512,1536]{0,1:T(8,128)(2,1)}, u32[]{:S(2)}, u32[]{:S(2)}) collective-permute-start(bf16[512,1536]{0,1:T(8,128)(2,1)} %bitcast.437), channel_id=1, source_target_pairs={{0,4},{4,0},{8,12},{12,8},{16,20},{20,16},{24,28},{28,24},{1,5},{5... | collective-permute-start | bytes 4718600 | tf_op jit(solution)/shard_map/ppermute | solution.py:42
  269.1 41.9 %collective-permute-start.39 = (bf16[512,1536]{0,1:T(8,128)(2,1)}, bf16[512,1536]{0,1:T(8,128)(2,1)}, u32[]{:S(2)}, u32[]{:S(2)}) collective-permute-start(bf16[512,1536]{0,1:T(8,128)(2,1)} %bitcast.111), channel_id=1, source_target_pairs={{0,4},{4,0},{8,12},{12,8},{16,20},{20,16},{24,28},{28,24},{1,5},{5... | collective-permute-start | bytes 4718600 | tf_op jit(solution)/shard_map/ppermute | solution.py:42
  310.4 118.0 %collective-permute-start.27 = (bf16[512,768]{1,0:T(8,128)(2,1)S(1)}, bf16[512,768]{1,0:T(8,128)(2,1)}, u32[]{:S(2)}, u32[]{:S(2)}) collective-permute-start(bf16[512,768]{1,0:T(8,128)(2,1)S(1)} %get-tuple-element.212), channel_id=1, source_target_pairs={{0,1},{1,2},{2,3},{3,0},{4,5},{5,6},{6,7},{7,4},{8,9},{9,10},{10,1... | collective-permute-start | bytes 2359304 | tf_op jit(solution)/shard_map/ppermute | solution.py:57
  311.3 117.9 %collective-permute-start.24 = (bf16[512,768]{1,0:T(8,128)(2,1)S(1)}, bf16[512,768]{1,0:T(8,128)(2,1)}, u32[]{:S(2)}, u32[]{:S(2)}) collective-permute-start(bf16[512,768]{1,0:T(8,128)(2,1)S(1)} %copy-done.42), channel_id=1, source_target_pairs={{0,1},{1,2},{2,3},{3,0},{4,5},{5,6},{6,7},{7,4},{8,9},{9,10},{10,1... | collective-permute-start | bytes 2359304 | tf_op jit(solution)/shard_map/ppermute | solution.py:57
  323.1 23.9 %collective-permute-start.44 = (bf16[2,2,96,768]{3,2,0,1:T(8,128)(2,1)S(1)}, bf16[2,2,96,768]{3,2,0,1:T(8,128)(2,1)S(1)}, u32[]{:S(2)}, u32[]{:S(2)}) collective-permute-start(bf16[2,2,96,768]{3,2,0,1:T(8,128)(2,1)S(1)} %bitcast.461), channel_id=1, source_target_pairs={{0,16},{4,20},{8,24},{12,28},{16,0},{20,4},{24,8},{28,12},{1,17},{... | collective-permute-start | bytes 1769480 | tf_op jit(solution)/shard_map/ppermute | solution.py:42
  335.1 23.1 %collective-permute-start.54 = (bf16[2,2,96,768]{3,2,0,1:T(8,128)(2,1)S(1)}, bf16[2,2,96,768]{3,2,0,1:T(8,128)(2,1)S(1)}, u32[]{:S(2)}, u32[]{:S(2)}) collective-permute-start(bf16[2,2,96,768]{3,2,0,1:T(8,128)(2,1)S(1)} %bitcast.465), channel_id=1, source_target_pairs={{0,16},{4,20},{8,24},{12,28},{16,0},{20,4},{24,8},{28,12},{1,17},{... | collective-permute-start | bytes 1769480 | tf_op jit(solution)/shard_map/ppermute | solution.py:42
  347.8 21.9 %collective-permute-start.36 = (bf16[2,96,768]{2,1,0:T(8,128)(2,1)S(1)}, bf16[2,96,768]{2,1,0:T(8,128)(2,1)S(1)}, u32[]{:S(2)}, u32[]{:S(2)}) collective-permute-start(bf16[2,96,768]{2,1,0:T(8,128)(2,1)S(1)} %dynamic-slice_bitcast_fusion.4), channel_id=1, source_target_pairs={{0,8},{4,12},{8,0},{12,4},{16,24},{20,28},{24,16},{28,20},{1,9},{5... | collective-permute-start | bytes 884744 | tf_op jit(solution)/shard_map/ppermute | solution.py:42
  428.4 31.4 %collective-permute-start.28 = (bf16[512,768]{1,0:T(8,128)(2,1)}, bf16[512,768]{1,0:T(8,128)(2,1)S(1)}, u32[]{:S(2)}, u32[]{:S(2)}) collective-permute-start(bf16[512,768]{1,0:T(8,128)(2,1)} %collective-permute-done.27), channel_id=1, source_target_pairs={{0,1},{1,2},{2,3},{3,0},{4,5},{5,6},{6,7},{7,4},{8,9},{9,10},{10,1... | collective-permute-start | bytes 2359304 | tf_op jit(solution)/shard_map/ppermute | solution.py:57
  429.2 33.0 %collective-permute-start.25 = (bf16[512,768]{1,0:T(8,128)(2,1)}, bf16[512,768]{1,0:T(8,128)(2,1)}, u32[]{:S(2)}, u32[]{:S(2)}) collective-permute-start(bf16[512,768]{1,0:T(8,128)(2,1)} %collective-permute-done.24), channel_id=1, source_target_pairs={{0,1},{1,2},{2,3},{3,0},{4,5},{5,6},{6,7},{7,4},{8,9},{9,10},{10,1... | collective-permute-start | bytes 2359304 | tf_op jit(solution)/shard_map/ppermute | solution.py:57
  434.1 62.9 %collective-permute-start.62 = (bf16[4,288,768]{2,1,0:T(8,128)(2,1)}, bf16[4,288,768]{2,1,0:T(8,128)(2,1)S(1)}, u32[]{:S(2)}, u32[]{:S(2)}) collective-permute-start(bf16[4,288,768]{2,1,0:T(8,128)(2,1)} %pad_maximum_fusion.6), channel_id=1, source_target_pairs={{0,4},{4,0},{8,12},{12,8},{16,20},{20,16},{24,28},{28,24},{1,5},{5... | collective-permute-start | bytes 5308424 | tf_op jit(solution)/shard_map/ppermute | solution.py:42
  459.8 23.3 %collective-permute-start.29 = (bf16[512,768]{1,0:T(8,128)(2,1)S(1)}, bf16[512,768]{1,0:T(8,128)(2,1)}, u32[]{:S(2)}, u32[]{:S(2)}) collective-permute-start(bf16[512,768]{1,0:T(8,128)(2,1)S(1)} %collective-permute-done.28), channel_id=1, source_target_pairs={{0,1},{1,2},{2,3},{3,0},{4,5},{5,6},{6,7},{7,4},{8,9},{9,10},{10,1... | collective-permute-start | bytes 2359304 | tf_op jit(solution)/shard_map/ppermute | solution.py:57
  462.2 32.8 %collective-permute-start.26 = (bf16[512,768]{1,0:T(8,128)(2,1)}, bf16[512,768]{1,0:T(8,128)(2,1)}, u32[]{:S(2)}, u32[]{:S(2)}) collective-permute-start(bf16[512,768]{1,0:T(8,128)(2,1)} %collective-permute-done.25), channel_id=1, source_target_pairs={{0,1},{1,2},{2,3},{3,0},{4,5},{5,6},{6,7},{7,4},{8,9},{9,10},{10,1... | collective-permute-start | bytes 2359304 | tf_op jit(solution)/shard_map/ppermute | solution.py:57
  (104 other events, 1093.1 us)
